TPU v7x, 128 devices: a whole 4x4x4 slice. The times are simulated.
128 devices in a mesh: row: 8 (over x_lo, z), col: 16 (over x_hi, y, core).
Axes of the slice: x: 4 (x_hi: 2, x_lo: 2; x = x_hi * 2 + x_lo), y: 4, z: 4, core: 2. Of those that a mesh axis runs over, the one named last changes fastest.
Arguments:
- tokens: bfloat16 [2048, 4096], P('row', 'col'), may hold values from -6 to 6
- norm_gain: float32 [4096], replicated, may hold values from 0.1 to 1.9
- expert_ids: int32 [2048, 2], P('row'), may hold values from 0 to 7, all different within a row; in each aligned block of 256 rows (0 to 255, 256 to 511, ...) at most 128 rows name the same one
- gate_weights: float32 [2048, 2], P('row'), may hold values from 0.1 to 1
- w_gate: bfloat16 [8, 4096, 14336], P('row', None, 'col'), may hold values from -0.09375 to 0.09375
- w_up: bfloat16 [8, 4096, 14336], P('row', None, 'col'), may hold values from -0.09375 to 0.09375
- w_down: bfloat16 [8, 14336, 4096], P('row', 'col'), may hold values from -0.046875 to 0.046875
Outputs:
- layer_output: bfloat16 [2048, 4096], P('row', 'col')
Inputs may be any that keep to these rules, and one draw needn't show every extreme that they name: `expert_ids`: the 2 experts of a token differ. In each aligned block of 256 tokens no expert is chosen by more than 128 tokens, a bound that some block reaches.
All inputs are finite; a program needn't handle non-finite values.
Results may differ from a plain program's by a relative error of at most 0.0043.
Values may be sent and summed in bfloat16 or wider, within the bound.
A program may use at most 128 MiB of HBM per device.

v0:
```python
import jax
import jax.numpy as jnp
from jax import lax
from jax.sharding import Mesh
from jax.sharding import PartitionSpec as P

EXPERTS = 8
CAP = 128
COL = ("chip", "core")


def route_tables(expert_ids, expert_count, capacity):
    token_count = expert_ids.shape[0]
    flat_ids = expert_ids.reshape(-1)
    expert_range = jnp.arange(expert_count, dtype=jnp.int32)
    expert_hits = (flat_ids[:, None] == expert_range[None, :]).astype(jnp.int32)
    earlier = jnp.cumsum(expert_hits, axis=0) - expert_hits
    ranks = jnp.sum(earlier * expert_hits, axis=1)
    slot_index = (flat_ids * capacity + ranks).reshape(token_count, -1)
    slot_ids = jnp.arange(expert_count * capacity, dtype=jnp.int32)
    matches = (slot_index[:, :, None] == slot_ids[None, None, :]).astype(jnp.float32)
    picker = jnp.sum(matches, axis=1)
    return (picker.astype(jnp.bfloat16), slot_index)


def combine_rows(slot_rows, slot_index, gate_weights):
    picked = slot_rows[slot_index]
    return jnp.sum(picked * gate_weights[:, :, None], axis=1)


def swap_cores(value):
    return lax.ppermute(value, "core", perm=[(0, 1), (1, 0)])


def body(tokens, norm_gain, expert_ids, gate_weights, w_gate, w_up, w_down):
    chips = lax.psum(1, "chip")
    width = tokens.shape[1]
    core = lax.axis_index("core")
    block = lax.axis_index("chip") * 2 + core
    values = tokens.astype(jnp.float32)
    squares = lax.psum(jnp.sum(values * values, axis=-1, keepdims=True), COL)
    inverse_norm = lax.rsqrt(squares / (width * chips * 2) + 1e-05)
    gain = lax.dynamic_slice_in_dim(norm_gain, block * width, width)
    normed = (values * inverse_norm * gain).astype(jnp.bfloat16)
    picker, slot_index = route_tables(expert_ids, EXPERTS, CAP)
    packed = jnp.einsum("ts,td->sd", picker, normed, preferred_element_type=jnp.float32).astype(
        jnp.bfloat16
    )
    packed = packed.reshape(EXPERTS, CAP, width)
    arrived = lax.all_to_all(packed, "row", split_axis=0, concat_axis=0, tiled=True)
    arrived = arrived.reshape(EXPERTS * CAP, width)
    mine = lax.all_gather(arrived, "chip", axis=0, tiled=False)
    other = swap_cores(mine)
    pair = jnp.where(core == 0, jnp.stack([mine, other], 1), jnp.stack([other, mine], 1))
    slots = arrived.shape[0]
    widened = jnp.transpose(pair, (2, 0, 1, 3)).reshape(slots, chips * 2 * width)
    gate_part = jnp.dot(widened, w_gate[0], preferred_element_type=jnp.float32)
    up_part = jnp.dot(widened, w_up[0], preferred_element_type=jnp.float32)
    hidden = (jax.nn.silu(gate_part) * up_part).astype(jnp.bfloat16)
    outputs = jnp.dot(hidden, w_down[0], preferred_element_type=jnp.float32)
    split = outputs.reshape(slots, chips, 2, width)
    keep = jnp.where(core == 0, split[:, :, 0], split[:, :, 1])
    give = jnp.where(core == 0, split[:, :, 1], split[:, :, 0])
    summed = keep + swap_cores(give)
    shares = lax.psum_scatter(summed, "chip", scatter_dimension=1, tiled=True)
    shares = shares.reshape(EXPERTS, CAP, width)
    returned = lax.all_to_all(shares, "row", split_axis=0, concat_axis=0, tiled=True)
    mixed = combine_rows(returned.reshape(-1, width), slot_index, gate_weights)
    return (tokens.astype(jnp.float32) + mixed).astype(jnp.bfloat16)


def solution(mesh):
    rows, cols = mesh.devices.shape
    split_mesh = Mesh(mesh.devices.reshape(rows, cols // 2, 2), ("row", "chip", "core"))
    placed = (
        P("row", COL),
        P(),
        P("row", None),
        P("row", None),
        P("row", None, COL),
        P("row", None, COL),
        P("row", COL, None),
    )
    return jax.shard_map(
        body, mesh=split_mesh, in_specs=placed, out_specs=P("row", COL), check_vma=False
    )
```

profile of v0, /device:TPU:0, one launch (start us, length us, event | category | flops | bytes accessed | tf_op | source)
XLA Modules:
  0.0 370.8 jit_solution(8695487437753940584)
XLA Ops:
  6.5 0.8 copy.51
  7.4 0.1 eq.48
  7.5 0.1 eq.44
  7.7 1.1 reduce-window.6
  8.8 0.2 slice_reduce_fusion
  9.2 0.1 reduce_sum.39
  9.4 0.7 compare_select_fusion
  10.1 0.3 convert_reduce_fusion
  10.4 1.0 fusion.9
  11.4 38.1 %psum.7 = f32[256,1]{0,1:T(1,128)S(1)} all-reduce(f32[256,1]{0,1:T(1,128)S(1)} %bitcast.67), channel_id=1, replica_groups=mesh['row'=8,'chip'=8,'core'=2] {'chip','core'}, use_global_device_ids=true, to_apply=%region_5.6 | all-reduce | flops 256 | bytes 2048 | tf_op jit(solution)/shard_map/psum | solution.py:41
  49.5 0.8 dynamic_slice.3
  50.3 1.3 convolution_convert_fusion
  51.6 13.9 %all_to_all.10 = bf16[8,128,256]{2,1,0:T(8,128)(2,1)} all-to-all(bf16[8,128,256]{2,1,0:T(8,128)(2,1)S(1)} %bitcast.66), channel_id=1, replica_groups=mesh['row'=8,'chip'=8,'core'=2] {'row'}, dimensions={0} | all-to-all | bytes 1048576 | tf_op jit(solution)/shard_map/all_to_all | solution.py:50
  65.5 67.0 %all-gather.2.cloned.1.call-done = bf16[8,1024,256]{2,1,0:T(8,128)(2,1)} async-done(((bf16[1,1024,256]{2,1,0:T(8,128)(2,1)}), bf16[8,1024,256]{2,1,0:T(8,128)(2,1)}) %all-gather.2.cloned.1.call-update) | async-done | bytes 4194320 | tf_op jit(solution)/shard_map/all_gather | solution.py:52
  132.6 6.4 %copy.54 = bf16[8,1024,256]{1,2,0:T(8,128)(2,1)} copy(bf16[8,1024,256]{2,1,0:T(8,128)(2,1)} %all-gather.2.cloned.1.call-done) | data formatting | bytes 8388608 | tf_op jit(solution)/shard_map/all_gather | solution.py:52
  139.0 10.8 %copy.64 = bf16[4096,896]{1,0:T(8,128)(2,1)} copy(bf16[4096,896]{0,1:T(8,128)(2,1)} %bitcast.60) | data formatting | bytes 14680064 | tf_op jit(solution)/shard_map/dot_general | solution.py:60
  149.8 7.9 %maximum_select_fusion = bf16[8,2,1024,256]{2,3,1,0:T(8,128)(2,1)S(1)} fusion(bf16[8,1,1024,256]{2,3,1,0:T(8,128)(2,1)} %bitcast.7, bf16[8,1,1024,256]{2,3,1,0:T(8,128)(2,1)} %bitcast.57, pred[]{:T(512)S(6)} %eq.43), kind=kLoop, calls=%fused_computation.1 | loop fusion | flops 12582912 | bytes 16777216 | tf_op jit(solution)/shard_map/jit(_where)/select_n | solution.py:54
  157.8 13.0 %fusion.2 = f32[1024,896]{1,0:T(8,128)S(1)} fusion(bf16[1024,4096]{0,1:T(8,128)(2,1)S(1)} %bitcast.58, bf16[1,4096,896]{2,1,0:T(8,128)(2,1)} %param.12), kind=kOutput, calls=%fused_computation.6 | convolution fusion | flops 7516192768 | bytes 19398656 | tf_op jit(solution)/shard_map/dot_general | solution.py:58
  170.9 11.1 %fusion.4 = f32[1024,896]{1,0:T(8,128)} fusion(bf16[1024,4096]{0,1:T(8,128)(2,1)S(1)} %bitcast.59, bf16[1,4096,896]{2,1,0:T(8,128)(2,1)S(1)} %bitcast.70), kind=kOutput, calls=%fused_computation.8 | convolution fusion | flops 7516192768 | bytes 19398656 | tf_op jit(solution)/shard_map/dot_general | solution.py:57
  182.0 13.8 %fusion.6 = f32[1024,8,2,256]{3,0,2,1:T(8,128)} fusion(bf16[8,2,256,896]{3,2,1,0:T(8,128)(2,1)S(1)} %bitcast.63, f32[1024,896]{1,0:T(8,128)S(1)} %fusion.2, f32[1024,896]{1,0:T(8,128)} %fusion.4), kind=kOutput, calls=%fused_computation.13 | convolution fusion | flops 7521697792 | bytes 31457280 | tf_op jit(solution)/shard_map/dot_general | solution.py:60
  195.8 10.1 %select_bitcast_fusion = f32[1024,8,256]{2,0,1:T(8,128)} fusion(f32[1024,8,2,256]{3,0,2,1:T(8,128)} %fusion.6, pred[]{:T(512)S(6)} %eq.43), kind=kLoop, calls=%fused_computation.5 | loop fusion | flops 2097152 | bytes 25165824 | tf_op jit(solution)/shard_map/jit(_where)/select_n | solution.py:63
  205.8 0.5 collective-permute-start.1
  206.3 13.0 %collective-permute-done.1 = f32[1024,8,256]{2,0,1:T(8,128)S(1)} collective-permute-done((f32[1024,8,256]{2,0,1:T(8,128)}, f32[1024,8,256]{2,0,1:T(8,128)S(1)}, u32[]{:S(2)}, u32[]{:S(2)}) %collective-permute-start.1) | collective-permute-done | bytes 8388640 | tf_op jit(solution)/shard_map/ppermute | solution.py:32
  219.3 10.0 %fusion.1 = f32[1024,8,256]{2,0,1:T(8,128)} fusion(f32[1024,8,256]{2,0,1:T(8,128)S(1)} %collective-permute-done.1, f32[1024,8,2,256]{3,0,2,1:T(8,128)} %fusion.6, pred[]{:T(512)S(6)} %eq.43), kind=kLoop, calls=%fused_computation.4 | loop fusion | flops 4194304 | bytes 33554432 | tf_op jit(solution)/shard_map/add | solution.py:64
  229.4 112.7 %reduce-scatter.2.cloned.1.call-done = f32[1024,1,256]{2,0,1:T(8,128)} async-done(((f32[1024,8,256]{2,0,1:T(8,128)}), f32[1024,1,256]{2,0,1:T(8,128)}) %reduce-scatter.2.cloned.1.call-update) | async-done | bytes 1048592 | tf_op jit(solution)/shard_map/reduce_scatter | solution.py:65
  342.1 4.4 %all-to-all-start.1 = ((f32[8,128,256]{2,1,0:T(8,128)}), f32[8,128,256]{2,1,0:T(8,128)S(1)}, u32[]{:S(2)}, u32[]{:S(2)}) async-start(f32[8,128,256]{2,1,0:T(8,128)} %bitcast.65), calls=%async_computation.2 | async-start | bytes 2097152 | tf_op jit(solution)/shard_map/all_to_all | solution.py:67
  346.6 0.1 reshape.53
  347.0 13.7 %all-to-all-done.1 = f32[8,128,256]{2,1,0:T(8,128)S(1)} async-done(((f32[8,128,256]{2,1,0:T(8,128)}), f32[8,128,256]{2,1,0:T(8,128)S(1)}, u32[]{:S(2)}, u32[]{:S(2)}) %all-to-all-start.1) | async-done | bytes 1048608 | tf_op jit(solution)/shard_map/all_to_all | solution.py:67
  360.7 1.6 gather_fusion
  362.3 0.3 reshape.52
  362.6 0.7 multiply_reduce_fusion
  363.3 0.7 fusion.12
  (29 shorter events, 0.6 us)
Async XLA Ops:
  6.5 126.0 %all-gather.2.cloned.1.call-start = ((), (), s32[]{:S(2)}) async-start(), calls=%async_computation.3 | async-start | bytes 4718592 | tf_op jit(solution)/shard_map/all_gather | solution.py:52
  65.5 276.6 %reduce-scatter.2.cloned.1.call-start = ((), (), s32[]{:S(2)}) async-start(), calls=%async_computation.4 | async-start | bytes 9437184 | tf_op jit(solution)/shard_map/reduce_scatter | solution.py:65
  139.0 10.8 %collective-permute-start = (bf16[8,1024,256]{1,2,0:T(8,128)(2,1)}, bf16[8,1024,256]{1,2,0:T(8,128)(2,1)}, u32[]{:S(2)}, u32[]{:S(2)}) collective-permute-start(bf16[8,1024,256]{1,2,0:T(8,128)(2,1)} %copy.54), channel_id=1, source_target_pairs={{0,1},{1,0},{2,3},{3,2},{4,5},{5,4},{6,7},{7,6},{8,9},{9,8},{10,11... | collective-permute-start | bytes 12582920 | tf_op jit(solution)/shard_map/ppermute | solution.py:32
  149.8 21.0 %slice-start.2 = ((s8[7340032]{0:T(1024)(128)(4,1)}), s8[4194304]{0:T(1024)(128)(4,1)S(1)}, s32[]{:S(2)}) async-start(s8[7340032]{0:T(1024)(128)(4,1)} %bitcast.69), calls=%async_computation.7 | async-start | bytes 8388608
  157.8 13.1 %slice-start.3 = ((s8[7340032]{0:T(1024)(128)(4,1)}), s8[3145728]{0:T(1024)(128)(4,1)S(1)}, s32[]{:S(2)}) async-start(s8[7340032]{0:T(1024)(128)(4,1)} %bitcast.69), calls=%async_computation.8 | async-start | bytes 6291456
  157.8 24.2 %slice-start = ((s8[7340032]{0:T(1024)(128)(4,1)}), s8[4194304]{0:T(1024)(128)(4,1)S(1)}, s32[]{:S(2)}) async-start(s8[7340032]{0:T(1024)(128)(4,1)} %bitcast.61), calls=%async_computation.5 | async-start | bytes 8388608
  170.9 11.1 %slice-start.1 = ((s8[7340032]{0:T(1024)(128)(4,1)}), s8[3145728]{0:T(1024)(128)(4,1)S(1)}, s32[]{:S(2)}) async-start(s8[7340032]{0:T(1024)(128)(4,1)} %bitcast.61), calls=%async_computation.6 | async-start | bytes 6291456
  205.8 13.5 %collective-permute-start.1 = (f32[1024,8,256]{2,0,1:T(8,128)}, f32[1024,8,256]{2,0,1:T(8,128)S(1)}, u32[]{:S(2)}, u32[]{:S(2)}) collective-permute-start(f32[1024,8,256]{2,0,1:T(8,128)} %select_bitcast_fusion), channel_id=1, source_target_pairs={{0,1},{1,0},{2,3},{3,2},{4,5},{5,4},{6,7},{7,6},{8,9},{9,8},{10,11... | collective-permute-start | bytes 25165832 | tf_op jit(solution)/shard_map/ppermute | solution.py:32
  229.3 117.4 %copy-start.1 = (f32[256,2]{0,1:T(2,128)S(1)}, f32[256,2]{0,1:T(2,128)}, u32[]{:S(2)}) copy-start(f32[256,2]{0,1:T(2,128)} %param.10) | copy-start | bytes 6148
  229.3 134.0 %copy-start = (bf16[256,256]{1,0:T(8,128)(2,1)S(1)}, bf16[256,256]{1,0:T(8,128)(2,1)}, u32[]{:S(2)}) copy-start(bf16[256,256]{1,0:T(8,128)(2,1)} %param.7) | copy-start | bytes 393220
  342.1 18.6 %all-to-all-start.1 = ((f32[8,128,256]{2,1,0:T(8,128)}), f32[8,128,256]{2,1,0:T(8,128)S(1)}, u32[]{:S(2)}, u32[]{:S(2)}) async-start(f32[8,128,256]{2,1,0:T(8,128)} %bitcast.65), calls=%async_computation.2 | async-start | bytes 2097152 | tf_op jit(solution)/shard_map/all_to_all | solution.py:67
Sparse Core Ops, SparseCore 0:
  65.6 66.8 all-gather.1
  229.5 112.5 reduce-scatter.1
where the time goes:
time: 372 us; the launch traced here: 371 us
  waiting for transfers between devices  206 us (55%)
  blocking collectives  52 us (14%)
  matrix products  39.2 us (11%)
  other arithmetic  32.7 us (9%)
  local copies, waits for them, and re-layouts  21.9 us (6%)
  between operations  13.6 us (4%)
  starting transfers between devices  4.98 us (1%)
    reduce_scatter x1, waiting for transfers between devices, body(): shares = lax.psum_scatter(summed, 'chip', scatter_dimension=1, tiled=True)  113 us
    all_gather x1, waiting for transfers between devices, body(): mine = lax.all_gather(arrived, 'chip', axis=0, tiled=False)  67 us
    psum x1, blocking collectives, body(): squares = lax.psum(jnp.sum(values * values, axis=-1, keepdims=True), COL)  38.1 us
    all_to_all x1, blocking collectives, body(): lax.all_to_all(packed, 'row', split_axis=0, concat_axis=0, tiled=True)  13.9 us
    dot_general x1, matrix products, body(): outputs = jnp.dot(hidden, w_down[0], preferred_element_type=jnp.float32)  13.8 us
    all_to_all x1, waiting for transfers between devices, body(): lax.all_to_all(shares, 'row', split_axis=0, concat_axis=0, tiled=True)  13.7 us
    dot_general x1, matrix products, body(): up_part = jnp.dot(widened, w_up[0], preferred_element_type=jnp.float32)  13 us
    ppermute x2, waiting for transfers between devices, swap_cores(): return lax.ppermute(value, 'core', perm=[(0, 1), (1, 0)])  13 us
  transfers between devices with their start and end apart: 5, of which 4 were waited for; matrix products, arithmetic and copies ran while one was open for 3% of the time, Pallas kernels for 0%

commit v1 on v0

--- a/solution.py
+++ b/solution.py
@@ -38,7 +38,9 @@
     core = lax.axis_index("core")
     block = lax.axis_index("chip") * 2 + core
     values = tokens.astype(jnp.float32)
-    squares = lax.psum(jnp.sum(values * values, axis=-1, keepdims=True), COL)
+    block_2 = jnp.sum(values * values, axis=-1, keepdims=True)
+    parts = lax.all_gather(block_2, COL, axis=0, tiled=False)
+    squares = parts.sum(axis=0)
     inverse_norm = lax.rsqrt(squares / (width * chips * 2) + 1e-05)
     gain = lax.dynamic_slice_in_dim(norm_gain, block * width, width)
     normed = (values * inverse_norm * gain).astype(jnp.bfloat16)

time: 372 us -> 360 us (0.968)
  blocking collectives: 52 us -> 40.2 us
    psum x1 -> x0, blocking collectives: 38.1 us -> none  [body(): squares = lax.psum(jnp.sum(values * values, axis=-1, keepdims=True), COL)]
    all_gather x0 -> x1, blocking collectives: none -> 24.5 us  [body(): parts = lax.all_gather(block_2, COL, axis=0, tiled=False)]
where the time goes in v1:
time: 360 us; the launch traced here: 359 us
  waiting for transfers between devices  206 us (57%)
  blocking collectives  40.2 us (11%)
  matrix products  39.2 us (11%)
  other arithmetic  32.7 us (9%)
  local copies, waits for them, and re-layouts  21.9 us (6%)
  between operations  13.6 us (4%)
  starting transfers between devices  4.99 us (1%)
    reduce_scatter x1, waiting for transfers between devices, body(): shares = lax.psum_scatter(summed, 'chip', scatter_dimension=1, tiled=True)  113 us
    all_gather x1, waiting for transfers between devices, body(): mine = lax.all_gather(arrived, 'chip', axis=0, tiled=False)  67.1 us
    all_gather x1, blocking collectives, body(): parts = lax.all_gather(block_2, COL, axis=0, tiled=False)  24.5 us
    all_to_all x1, blocking collectives, body(): lax.all_to_all(packed, 'row', split_axis=0, concat_axis=0, tiled=True)  15.7 us
    dot_general x1, matrix products, body(): outputs = jnp.dot(hidden, w_down[0], preferred_element_type=jnp.float32)  13.8 us
    all_to_all x1, waiting for transfers between devices, body(): lax.all_to_all(shares, 'row', split_axis=0, concat_axis=0, tiled=True)  13.8 us
    dot_general x1, matrix products, body(): up_part = jnp.dot(widened, w_up[0], preferred_element_type=jnp.float32)  13 us
    ppermute x2, waiting for transfers between devices, swap_cores(): return lax.ppermute(value, 'core', perm=[(0, 1), (1, 0)])  13 us
  transfers between devices with their start and end apart: 5, of which 4 were waited for; matrix products, arithmetic and copies ran while one was open for 3% of the time, Pallas kernels for 0%

profile of v1, /device:TPU:0, one launch (start us, length us, event | category | flops | bytes accessed | tf_op | source)
XLA Modules:
  0.0 359.1 jit_solution(1768835045597545297)
XLA Ops:
  6.5 0.8 copy.51
  7.4 0.1 eq.48
  7.5 0.1 eq.44
  7.7 1.1 reduce-window.6
  8.8 0.2 slice_reduce_fusion
  9.2 0.1 reduce_sum.48
  9.4 0.7 compare_select_fusion
  10.1 0.3 convert_reduce_fusion
  10.4 1.0 fusion.9
  11.4 24.5 %all-gather.1 = f32[16,1,256]{2,1,0:T(1,128)S(1)} all-gather(f32[1,1,256]{2,1,0:T(1,128)S(1)} %bitcast.66), channel_id=2, replica_groups=mesh['row'=8,'chip'=8,'core'=2] {'chip','core'}, dimensions={0}, use_global_device_ids=true | all-gather | bytes 17408 | tf_op jit(solution)/shard_map/all_gather | solution.py:42
  35.9 0.8 dynamic_slice.3
  36.7 1.3 convolution_convert_fusion
  38.0 15.7 %all_to_all.10 = bf16[8,128,256]{2,1,0:T(8,128)(2,1)} all-to-all(bf16[8,128,256]{2,1,0:T(8,128)(2,1)S(1)} %bitcast.65), channel_id=1, replica_groups=mesh['row'=8,'chip'=8,'core'=2] {'row'}, dimensions={0} | all-to-all | bytes 1048576 | tf_op jit(solution)/shard_map/all_to_all | solution.py:52
  53.8 67.1 %all-gather.4.cloned.1.call-done = bf16[8,1024,256]{2,1,0:T(8,128)(2,1)} async-done(((bf16[1,1024,256]{2,1,0:T(8,128)(2,1)}), bf16[8,1024,256]{2,1,0:T(8,128)(2,1)}) %all-gather.4.cloned.1.call-update) | async-done | bytes 4194320 | tf_op jit(solution)/shard_map/all_gather | solution.py:54
  120.8 6.4 %copy.54 = bf16[8,1024,256]{1,2,0:T(8,128)(2,1)} copy(bf16[8,1024,256]{2,1,0:T(8,128)(2,1)} %all-gather.4.cloned.1.call-done) | data formatting | bytes 8388608 | tf_op jit(solution)/shard_map/all_gather | solution.py:54
  127.3 10.8 %copy.64 = bf16[4096,896]{1,0:T(8,128)(2,1)} copy(bf16[4096,896]{0,1:T(8,128)(2,1)} %bitcast.59) | data formatting | bytes 14680064 | tf_op jit(solution)/shard_map/dot_general | solution.py:62
  138.1 7.9 %maximum_select_fusion = bf16[8,2,1024,256]{2,3,1,0:T(8,128)(2,1)S(1)} fusion(bf16[8,1,1024,256]{2,3,1,0:T(8,128)(2,1)} %bitcast.6, bf16[8,1,1024,256]{2,3,1,0:T(8,128)(2,1)} %bitcast.56, pred[]{:T(512)S(6)} %eq.43), kind=kLoop, calls=%fused_computation.1 | loop fusion | flops 12582912 | bytes 16777216 | tf_op jit(solution)/shard_map/jit(_where)/select_n | solution.py:56
  146.1 13.0 %fusion.2 = f32[1024,896]{1,0:T(8,128)S(1)} fusion(bf16[1024,4096]{0,1:T(8,128)(2,1)S(1)} %bitcast.57, bf16[1,4096,896]{2,1,0:T(8,128)(2,1)} %param.12), kind=kOutput, calls=%fused_computation.6 | convolution fusion | flops 7516192768 | bytes 19398656 | tf_op jit(solution)/shard_map/dot_general | solution.py:60
  159.1 11.1 %fusion.4 = f32[1024,896]{1,0:T(8,128)} fusion(bf16[1024,4096]{0,1:T(8,128)(2,1)S(1)} %bitcast.58, bf16[1,4096,896]{2,1,0:T(8,128)(2,1)S(1)} %bitcast.68), kind=kOutput, calls=%fused_computation.8 | convolution fusion | flops 7516192768 | bytes 19398656 | tf_op jit(solution)/shard_map/dot_general | solution.py:59
  170.2 13.8 %fusion.6 = f32[1024,8,2,256]{3,0,2,1:T(8,128)} fusion(bf16[8,2,256,896]{3,2,1,0:T(8,128)(2,1)S(1)} %bitcast.62, f32[1024,896]{1,0:T(8,128)S(1)} %fusion.2, f32[1024,896]{1,0:T(8,128)} %fusion.4), kind=kOutput, calls=%fused_computation.13 | convolution fusion | flops 7521697792 | bytes 31457280 | tf_op jit(solution)/shard_map/dot_general | solution.py:62
  184.0 10.1 %select_bitcast_fusion = f32[1024,8,256]{2,0,1:T(8,128)} fusion(f32[1024,8,2,256]{3,0,2,1:T(8,128)} %fusion.6, pred[]{:T(512)S(6)} %eq.43), kind=kLoop, calls=%fused_computation.5 | loop fusion | flops 2097152 | bytes 25165824 | tf_op jit(solution)/shard_map/jit(_where)/select_n | solution.py:65
  194.1 0.5 collective-permute-start.1
  194.6 13.0 %collective-permute-done.1 = f32[1024,8,256]{2,0,1:T(8,128)S(1)} collective-permute-done((f32[1024,8,256]{2,0,1:T(8,128)}, f32[1024,8,256]{2,0,1:T(8,128)S(1)}, u32[]{:S(2)}, u32[]{:S(2)}) %collective-permute-start.1) | collective-permute-done | bytes 8388640 | tf_op jit(solution)/shard_map/ppermute | solution.py:32
  207.6 10.0 %fusion.1 = f32[1024,8,256]{2,0,1:T(8,128)} fusion(f32[1024,8,256]{2,0,1:T(8,128)S(1)} %collective-permute-done.1, f32[1024,8,2,256]{3,0,2,1:T(8,128)} %fusion.6, pred[]{:T(512)S(6)} %eq.43), kind=kLoop, calls=%fused_computation.4 | loop fusion | flops 4194304 | bytes 33554432 | tf_op jit(solution)/shard_map/add | solution.py:66
  217.6 112.6 %reduce-scatter.2.cloned.1.call-done = f32[1024,1,256]{2,0,1:T(8,128)} async-done(((f32[1024,8,256]{2,0,1:T(8,128)}), f32[1024,1,256]{2,0,1:T(8,128)}) %reduce-scatter.2.cloned.1.call-update) | async-done | bytes 1048592 | tf_op jit(solution)/shard_map/reduce_scatter | solution.py:67
  330.3 4.4 %all-to-all-start.1 = ((f32[8,128,256]{2,1,0:T(8,128)}), f32[8,128,256]{2,1,0:T(8,128)S(1)}, u32[]{:S(2)}, u32[]{:S(2)}) async-start(f32[8,128,256]{2,1,0:T(8,128)} %bitcast.64), calls=%async_computation.2 | async-start | bytes 2097152 | tf_op jit(solution)/shard_map/all_to_all | solution.py:69
  334.9 0.1 reshape.62
  335.2 13.8 %all-to-all-done.1 = f32[8,128,256]{2,1,0:T(8,128)S(1)} async-done(((f32[8,128,256]{2,1,0:T(8,128)}), f32[8,128,256]{2,1,0:T(8,128)S(1)}, u32[]{:S(2)}, u32[]{:S(2)}) %all-to-all-start.1) | async-done | bytes 1048608 | tf_op jit(solution)/shard_map/all_to_all | solution.py:69
  348.9 1.6 gather_fusion
  350.5 0.3 reshape.61
  350.8 0.7 multiply_reduce_fusion
  351.5 0.7 fusion.12
  (30 shorter events, 0.6 us)
Async XLA Ops:
  6.5 114.3 %all-gather.4.cloned.1.call-start = ((), (), s32[]{:S(2)}) async-start(), calls=%async_computation.3 | async-start | bytes 4718592 | tf_op jit(solution)/shard_map/all_gather | solution.py:54
  53.7 276.6 %reduce-scatter.2.cloned.1.call-start = ((), (), s32[]{:S(2)}) async-start(), calls=%async_computation.4 | async-start | bytes 9437184 | tf_op jit(solution)/shard_map/reduce_scatter | solution.py:67
  127.3 10.8 %collective-permute-start = (bf16[8,1024,256]{1,2,0:T(8,128)(2,1)}, bf16[8,1024,256]{1,2,0:T(8,128)(2,1)}, u32[]{:S(2)}, u32[]{:S(2)}) collective-permute-start(bf16[8,1024,256]{1,2,0:T(8,128)(2,1)} %copy.54), channel_id=1, source_target_pairs={{0,1},{1,0},{2,3},{3,2},{4,5},{5,4},{6,7},{7,6},{8,9},{9,8},{10,11... | collective-permute-start | bytes 12582920 | tf_op jit(solution)/shard_map/ppermute | solution.py:32
  138.1 21.0 %slice-start.2 = ((s8[7340032]{0:T(1024)(128)(4,1)}), s8[4194304]{0:T(1024)(128)(4,1)S(1)}, s32[]{:S(2)}) async-start(s8[7340032]{0:T(1024)(128)(4,1)} %bitcast.67), calls=%async_computation.7 | async-start | bytes 8388608
  146.0 13.1 %slice-start.3 = ((s8[7340032]{0:T(1024)(128)(4,1)}), s8[3145728]{0:T(1024)(128)(4,1)S(1)}, s32[]{:S(2)}) async-start(s8[7340032]{0:T(1024)(128)(4,1)} %bitcast.67), calls=%async_computation.8 | async-start | bytes 6291456
  146.1 24.2 %slice-start = ((s8[7340032]{0:T(1024)(128)(4,1)}), s8[4194304]{0:T(1024)(128)(4,1)S(1)}, s32[]{:S(2)}) async-start(s8[7340032]{0:T(1024)(128)(4,1)} %bitcast.60), calls=%async_computation.5 | async-start | bytes 8388608
  159.1 11.1 %slice-start.1 = ((s8[7340032]{0:T(1024)(128)(4,1)}), s8[3145728]{0:T(1024)(128)(4,1)S(1)}, s32[]{:S(2)}) async-start(s8[7340032]{0:T(1024)(128)(4,1)} %bitcast.60), calls=%async_computation.6 | async-start | bytes 6291456
  194.1 13.5 %collective-permute-start.1 = (f32[1024,8,256]{2,0,1:T(8,128)}, f32[1024,8,256]{2,0,1:T(8,128)S(1)}, u32[]{:S(2)}, u32[]{:S(2)}) collective-permute-start(f32[1024,8,256]{2,0,1:T(8,128)} %select_bitcast_fusion), channel_id=1, source_target_pairs={{0,1},{1,0},{2,3},{3,2},{4,5},{5,4},{6,7},{7,6},{8,9},{9,8},{10,11... | collective-permute-start | bytes 25165832 | tf_op jit(solution)/shard_map/ppermute | solution.py:32
  217.6 117.4 %copy-start.1 = (f32[256,2]{0,1:T(2,128)S(1)}, f32[256,2]{0,1:T(2,128)}, u32[]{:S(2)}) copy-start(f32[256,2]{0,1:T(2,128)} %param.10) | copy-start | bytes 6148
  217.6 133.9 %copy-start = (bf16[256,256]{1,0:T(8,128)(2,1)S(1)}, bf16[256,256]{1,0:T(8,128)(2,1)}, u32[]{:S(2)}) copy-start(bf16[256,256]{1,0:T(8,128)(2,1)} %param.7) | copy-start | bytes 393220
  330.3 18.7 %all-to-all-start.1 = ((f32[8,128,256]{2,1,0:T(8,128)}), f32[8,128,256]{2,1,0:T(8,128)S(1)}, u32[]{:S(2)}, u32[]{:S(2)}) async-start(f32[8,128,256]{2,1,0:T(8,128)} %bitcast.64), calls=%async_computation.2 | async-start | bytes 2097152 | tf_op jit(solution)/shard_map/all_to_all | solution.py:69
Sparse Core Ops, SparseCore 0:
  53.8 66.9 all-gather.3
  217.8 112.4 reduce-scatter.1
